TPU v7x, 32 devices: a whole 2x2x4 slice. The times are simulated.
32 devices in a mesh: row: 8 (over z, core), col: 4 (over y, x).
Axes of the slice: x: 2, y: 2, z: 4, core: 2. Of those that a mesh axis runs over, the one named last changes fastest.
Arguments:
- similarity: bfloat16 [2048, 2048], P('row', 'col')
- in_mask: int32 [8, 8], P('row', 'col'), may hold values from 0 to 1, as said below
- out_mask: int32 [8, 8], P('row', 'col'), may hold values from 0 to 1, as said below
Outputs:
- stochastic: float32 [2048, 2048], P('row', 'col')
Inputs may be any that keep to these rules, and one draw needn't show every extreme that they name: in_mask is symmetric, similarity is symmetric and nonnegative with positive diagonal entries, and every diagonal block is present. `out_mask`: every diagonal block is kept.
All inputs are finite; a program needn't handle non-finite values.
Results may differ from a plain program's by a relative error of at most 0.0003.
Values may be sent and summed in bfloat16 or wider, within the bound.
No kernel may reach another device: no remote copies, remote signals or barrier semaphores. Data moves between devices by JAX's collectives and lax.ppermute only.
A program may use at most 64 MiB of HBM per device.

v0:
```python
import jax
import jax.numpy as jnp
from jax import lax
from jax.sharding import PartitionSpec as P

BS = 256


def on_device(similarity, in_mask, out_mask):
    rows_loc, cols_loc = similarity.shape
    rblocks, cblocks = in_mask.shape
    live = in_mask.astype(jnp.bfloat16)[:, None, :, None]
    sparse = (similarity.reshape(rblocks, BS, cblocks, BS) * live).reshape(rows_loc, cols_loc)
    row_panel = lax.all_gather(sparse, "col", axis=1, tiled=True)
    product = jnp.dot(
        row_panel,
        lax.all_gather(sparse, "row", axis=0, tiled=True),
        preferred_element_type=jnp.float32,
    )
    keep = out_mask.astype(jnp.float32)[:, None, :, None]
    kept = (product.reshape(rblocks, BS, cblocks, BS) * keep).reshape(rows_loc, cols_loc)
    inflated = kept * kept
    column_sums = lax.psum(jnp.sum(inflated, axis=0), "row")
    total = jnp.float32(rows_loc * lax.axis_size("row"))
    return inflated * (total / column_sums)[None, :]


def solution(mesh):
    in_specs = (P("row", "col"), P("row", "col"), P("row", "col"))
    out_specs = P("row", "col")
    return jax.shard_map(
        on_device, mesh=mesh, in_specs=in_specs, out_specs=out_specs, check_vma=False
    )
```

profile of v0, /device:TPU:0, one launch (start us, length us, event | category | flops | bytes accessed | tf_op | source)
XLA Modules:
  0.0 94.9 jit_solution(12435030798267104924)
XLA Ops:
  6.5 0.0 all-gather.3.cloned.1.call-start
  6.5 0.7 convert_bitcast_fusion.1
  7.2 0.1 broadcast_bitcast_fusion.1
  7.3 1.7 %broadcast_multiply_fusion.1 = bf16[256,512]{1,0:T(8,128)(2,1)} fusion(bf16[256,512]{1,0:T(8,128)(2,1)} %param.3, bf16[512]{0:T(512)(128)(2,1)S(1)} %bitcast.12), kind=kLoop, calls=%fused_computation.3 | loop fusion | flops 131072 | bytes 525312 | tf_op jit(solution)/shard_map/mul | solution.py:13
  9.0 0.0 all-gather.3.cloned.1.call-update
  9.0 0.0 all-gather.5.cloned.1.call-start
  9.0 0.7 all-gather.5.cloned.1.call-update
  9.7 0.7 convert_bitcast_fusion
  10.4 0.1 broadcast_bitcast_fusion
  10.5 27.9 %all-gather.3.cloned.1.call-done = bf16[256,2048]{1,0:T(8,128)(2,1)} async-done(((bf16[256,512]{1,0:T(8,128)(2,1)}), bf16[256,2048]{1,0:T(8,128)(2,1)}) %all-gather.3.cloned.1.call-update) | async-done | bytes 1048592 | tf_op jit(solution)/shard_map/all_gather | solution.py:14
  38.4 30.7 %all-gather.5.cloned.1.call-done = bf16[2048,512]{1,0:T(8,128)(2,1)} async-done(((bf16[256,512]{1,0:T(8,128)(2,1)}), bf16[2048,512]{1,0:T(8,128)(2,1)}) %all-gather.5.cloned.1.call-update) | async-done | bytes 2097168 | tf_op jit(solution)/shard_map/all_gather | solution.py:17
  69.1 2.6 %fusion.1 = (f32[512]{0:T(512)S(1)}, f32[256,512]{1,0:T(8,128)S(1)}) fusion(f32[512]{0:T(512)S(1)} %bitcast.13, bf16[256,2048]{1,0:T(8,128)(2,1)} %all-gather.3.cloned.1.call-done, bf16[2048,512]{1,0:T(8,128)(2,1)} %all-gather.5.cloned.1.call-done), kind=kOutput, calls=%fused_computation.9 | convolution fusion | flops 537263616 | bytes 3674112 | tf_op jit(solution)/shard_map/dot_general | solution.py:15
  71.8 15.4 %psum.7 = f32[512]{0:T(512)S(1)} all-reduce(f32[512]{0:T(512)S(1)} %get-tuple-element.5), channel_id=1, replica_groups=mesh['row'=8,'col'=4] {'row'}, use_global_device_ids=true, to_apply=%region_1.0 | all-reduce | flops 512 | bytes 4096 | tf_op jit(solution)/shard_map/psum | solution.py:23
  87.2 0.9 broadcast_multiply_fusion
  (3 shorter events, 0.0 us)
Async XLA Ops:
  6.5 31.9 %all-gather.3.cloned.1.call-start = ((), (), s32[]{:S(2)}) async-start(), calls=%async_computation | async-start | bytes 1310720 | tf_op jit(solution)/shard_map/all_gather | solution.py:14
  9.0 60.2 %all-gather.5.cloned.1.call-start = ((), (), s32[]{:S(2)}) async-start(), calls=%async_computation.1 | async-start | bytes 2359296 | tf_op jit(solution)/shard_map/all_gather | solution.py:17
Sparse Core Ops, SparseCore 0:
  9.2 29.1 all-gather.2
  40.0 29.0 all-gather.4
where the time goes:
time: 95.1 us; the launch traced here: 94.9 us
  waiting for transfers between devices  59.4 us (62%)
  blocking collectives  15.4 us (16%)
  between operations  13.4 us (14%)
  other arithmetic  3.87 us (4%)
  matrix products  2.64 us (3%)
    all_gather x1, waiting for transfers between devices, on_device(): lax.all_gather(sparse, 'row', axis=0, tiled=True)  30.7 us
    all_gather x1, waiting for transfers between devices, on_device(): row_panel = lax.all_gather(sparse, 'col', axis=1, tiled=True)  27.9 us
    psum x1, blocking collectives, on_device(): column_sums = lax.psum(jnp.sum(inflated, axis=0), 'row')  15.4 us
    dot_general x1, matrix products, on_device(): jnp.dot(row_panel, lax.all_gather(sparse, 'row', axis=0, tiled=True), pre...  2.64 us
    mul x2, other arithmetic, on_device(): similarity.reshape(rblocks, BS, cblocks, BS) * live  2.33 us
  transfers between devices with their start and end apart: 2, of which 2 were waited for; matrix products, arithmetic and copies ran while one was open for 1% of the time, Pallas kernels for 0%

commit v1 on v0

--- a/solution.py
+++ b/solution.py
@@ -4,6 +4,19 @@
 from jax.sharding import PartitionSpec as P
 
 BS = 256
+
+
+def gather_around(value, axis, dim):
+    ways = lax.axis_size(axis)
+    up = [(d, (d + 1) % ways) for d in range(ways)]
+    down = [(d, (d - 1) % ways) for d in range(ways)]
+    earlier, later = ([value], [value])
+    for _ in range(ways // 2):
+        earlier.append(lax.ppermute(earlier[-1], axis, up))
+    for _ in range((ways - 1) // 2):
+        later.append(lax.ppermute(later[-1], axis, down))
+    line = jnp.concatenate([*earlier[::-1], *later[1:]], axis=dim)
+    return jnp.roll(line, (lax.axis_index(axis) - ways // 2) * value.shape[dim], axis=dim)
 
 
 def on_device(similarity, in_mask, out_mask):
@@ -13,9 +26,7 @@
     sparse = (similarity.reshape(rblocks, BS, cblocks, BS) * live).reshape(rows_loc, cols_loc)
     row_panel = lax.all_gather(sparse, "col", axis=1, tiled=True)
     product = jnp.dot(
-        row_panel,
-        lax.all_gather(sparse, "row", axis=0, tiled=True),
-        preferred_element_type=jnp.float32,
+        row_panel, gather_around(sparse, "row", 0), preferred_element_type=jnp.float32
     )
     keep = out_mask.astype(jnp.float32)[:, None, :, None]
     kept = (product.reshape(rblocks, BS, cblocks, BS) * keep).reshape(rows_loc, cols_loc)

time: 95.1 us -> 82.3 us (0.87)
  waiting for transfers between devices: 59.4 us -> 24.2 us
  starting transfers between devices: 0.04 us -> 11.2 us
  local copies, waits for them, and re-layouts: 0.16 us -> 10.2 us
  other arithmetic: 3.87 us -> 5.66 us
    all_gather x1 -> x0, waiting for transfers between devices: 30.7 us -> none  [on_device(): lax.all_gather(sparse, 'row', axis=0, tiled=True)]
    all_gather x1, waiting for transfers between devices: 27.9 us -> 0.01 us  [on_device(): row_panel = lax.all_gather(sparse, 'col', axis=1, tiled=True)]
    ppermute x0 -> x7, waiting for transfers between devices: none -> 24.1 us  [the longest x4 24.1 us: gather_around(): earlier.append(lax.ppermute(earlier[-1], axis, up))]
    ppermute x0 -> x7, starting transfers between devices: none -> 11.2 us  [the longest x3 10.7 us: gather_around(): later.append(lax.ppermute(later[-1], axis, down))]
    unnamed x4 -> x21, local copies, waits for them, and re-layouts: 0.16 us -> 9.45 us
    unnamed x0 -> x2, other arithmetic: none -> 2.45 us
  transfers between devices with their start and end apart: 2 -> 8, of which waited for: 2 -> 4; matrix products, arithmetic and copies ran while one was open for 1% -> 16% of each run, Pallas kernels for 0% -> 0%
where the time goes in v1:
time: 82.3 us; the launch traced here: 82.1 us
  waiting for transfers between devices  24.2 us (29%)
  blocking collectives  14.9 us (18%)
  between operations  13.4 us (16%)
  starting transfers between devices  11.2 us (14%)
  local copies, waits for them, and re-layouts  10.2 us (12%)
  other arithmetic  5.66 us (7%)
  matrix products  2.64 us (3%)
    ppermute x4, waiting for transfers between devices, gather_around(): earlier.append(lax.ppermute(earlier[-1], axis, up))  24.1 us
    psum x1, blocking collectives, on_device(): column_sums = lax.psum(jnp.sum(inflated, axis=0), 'row')  14.9 us
    ppermute x3, starting transfers between devices, gather_around(): later.append(lax.ppermute(later[-1], axis, down))  10.7 us
    unnamed x21, local copies, waits for them, and re-layouts  9.45 us
    dot_general x1, matrix products, on_device(): jnp.dot(row_panel, gather_around(sparse, 'row', 0), preferred_element_typ...  2.64 us
    unnamed x2, other arithmetic  2.45 us
    mul x2, other arithmetic, on_device(): similarity.reshape(rblocks, BS, cblocks, BS) * live  1.67 us
  transfers between devices with their start and end apart: 8, of which 4 were waited for; matrix products, arithmetic and copies ran while one was open for 16% of the time, Pallas kernels for 0%

profile of v1, /device:TPU:0, one launch (start us, length us, event | category | flops | bytes accessed | tf_op | source)
XLA Modules:
  0.0 82.1 jit_solution(11573594308289691060)
XLA Ops:
  6.5 0.7 convert_bitcast_fusion.1
  7.2 0.1 broadcast_bitcast_fusion.1
  7.3 1.0 %broadcast_multiply_fusion.1 = bf16[256,512]{1,0:T(8,128)(2,1)S(1)} fusion(bf16[256,512]{1,0:T(8,128)(2,1)} %param.3, bf16[512]{0:T(512)(128)(2,1)S(1)} %bitcast.11), kind=kLoop, calls=%fused_computation.5 | loop fusion | flops 131072 | bytes 525312 | tf_op jit(solution)/shard_map/mul | solution.py:26
  8.3 0.5 collective-permute-start
  8.8 8.1 %collective-permute-done = bf16[256,512]{1,0:T(8,128)(2,1)S(1)} collective-permute-done((bf16[256,512]{1,0:T(8,128)(2,1)S(1)}, bf16[256,512]{1,0:T(8,128)(2,1)S(1)}, u32[]{:S(2)}, u32[]{:S(2)}) %collective-permute-start) | collective-permute-done | bytes 262176 | tf_op jit(solution)/shard_map/ppermute | solution.py:15
  16.9 3.5 %collective-permute-start.4 = (bf16[256,512]{1,0:T(8,128)(2,1)S(1)}, bf16[256,512]{1,0:T(8,128)(2,1)S(1)}, u32[]{:S(2)}, u32[]{:S(2)}) collective-permute-start(bf16[256,512]{1,0:T(8,128)(2,1)S(1)} %broadcast_multiply_fusion.1), channel_id=1, source_target_pairs={{0,28},{4,0},{8,4},{12,8},{16,12},{20,16},{24,20},{28,24},{1,29},{... | collective-permute-start | bytes 786440 | tf_op jit(solution)/shard_map/ppermute | solution.py:17
  20.5 6.1 %collective-permute-done.1 = bf16[256,512]{1,0:T(8,128)(2,1)S(1)} collective-permute-done((bf16[256,512]{1,0:T(8,128)(2,1)S(1)}, bf16[256,512]{1,0:T(8,128)(2,1)S(1)}, u32[]{:S(2)}, u32[]{:S(2)}) %collective-permute-start.1) | collective-permute-done | bytes 262176 | tf_op jit(solution)/shard_map/ppermute | solution.py:15
  26.6 3.6 %collective-permute-start.5 = (bf16[256,512]{1,0:T(8,128)(2,1)S(1)}, bf16[256,512]{1,0:T(8,128)(2,1)S(1)}, u32[]{:S(2)}, u32[]{:S(2)}) collective-permute-start(bf16[256,512]{1,0:T(8,128)(2,1)S(1)} %collective-permute-done.4), channel_id=1, source_target_pairs={{0,28},{4,0},{8,4},{12,8},{16,12},{20,16},{24,20},{28,24},{1,29},{... | collective-permute-start | bytes 786440 | tf_op jit(solution)/shard_map/ppermute | solution.py:17
  30.2 6.1 %collective-permute-done.2 = bf16[256,512]{1,0:T(8,128)(2,1)S(1)} collective-permute-done((bf16[256,512]{1,0:T(8,128)(2,1)S(1)}, bf16[256,512]{1,0:T(8,128)(2,1)S(1)}, u32[]{:S(2)}, u32[]{:S(2)}) %collective-permute-start.2) | collective-permute-done | bytes 262176 | tf_op jit(solution)/shard_map/ppermute | solution.py:15
  36.3 0.7 convert_bitcast_fusion
  36.9 0.1 broadcast_bitcast_fusion
  37.0 3.5 %collective-permute-start.6 = (bf16[256,512]{1,0:T(8,128)(2,1)S(1)}, bf16[256,512]{1,0:T(8,128)(2,1)S(1)}, u32[]{:S(2)}, u32[]{:S(2)}) collective-permute-start(bf16[256,512]{1,0:T(8,128)(2,1)S(1)} %collective-permute-done.5), channel_id=1, source_target_pairs={{0,28},{4,0},{8,4},{12,8},{16,12},{20,16},{24,20},{28,24},{1,29},{... | collective-permute-start | bytes 786440 | tf_op jit(solution)/shard_map/ppermute | solution.py:17
  40.6 3.9 %collective-permute-done.3 = bf16[256,512]{1,0:T(8,128)(2,1)S(1)} collective-permute-done((bf16[256,512]{1,0:T(8,128)(2,1)S(1)}, bf16[256,512]{1,0:T(8,128)(2,1)S(1)}, u32[]{:S(2)}, u32[]{:S(2)}) %collective-permute-start.3) | collective-permute-done | bytes 262176 | tf_op jit(solution)/shard_map/ppermute | solution.py:15
  44.4 0.7 constant_dynamic-update-slice_fusion.15
  45.1 0.7 constant_dynamic-update-slice_fusion.14
  45.8 0.7 constant_dynamic-update-slice_fusion.13
  46.6 0.7 constant_dynamic-update-slice_fusion.12
  47.3 1.7 %constant_dynamic-update-slice_fusion.11 = bf16[4096,512]{1,0:T(8,128)(2,1)} fusion(bf16[4096,512]{1,0:T(8,128)(2,1)} %constant_dynamic-update-slice_fusion.12, bf16[256,512]{1,0:T(8,128)(2,1)} %param.3, bf16[512]{0:T(512)(128)(2,1)S(1)} %bitcast.12), kind=kLoop, calls=%fused_computation.17 | loop fusion | flops 524288 | bytes 525312
  49.0 0.7 constant_dynamic-update-slice_fusion.10
  49.7 0.7 constant_dynamic-update-slice_fusion.9
  50.4 0.7 constant_dynamic-update-slice_fusion.8
  51.1 0.7 constant_dynamic-update-slice_fusion.7
  51.8 0.7 constant_dynamic-update-slice_fusion.6
  52.5 0.7 constant_dynamic-update-slice_fusion.5
  53.3 0.7 constant_dynamic-update-slice_fusion.4
  54.0 0.7 constant_dynamic-update-slice_fusion.3
  54.8 0.7 constant_dynamic-update-slice_fusion.2
  55.5 0.7 constant_dynamic-update-slice_fusion.1
  56.2 0.7 constant_dynamic-update-slice_fusion
  56.9 2.6 %fusion.9 = (f32[512]{0:T(512)S(1)}, f32[256,512]{1,0:T(8,128)S(1)}) fusion(f32[512]{0:T(512)S(1)} %bitcast.14, bf16[256,2048]{1,0:T(8,128)(2,1)} %all-gather.2.cloned.1.call-done, bf16[4096,512]{1,0:T(8,128)(2,1)} %constant_dynamic-update-slice_fusion, s32[]{:T(128)S(6)} %select_n.14), kind=kOutput, calls=%fused_computation.28 | convolution fusion | flops 537263616 | bytes 3674116 | tf_op jit(solution)/shard_map/dot_general | solution.py:28
  59.5 14.9 %psum.7 = f32[512]{0:T(512)S(1)} all-reduce(f32[512]{0:T(512)S(1)} %get-tuple-element.5), channel_id=1, replica_groups=mesh['row'=8,'col'=4] {'row'}, use_global_device_ids=true, to_apply=%region_1.2 | all-reduce | flops 512 | bytes 4096 | tf_op jit(solution)/shard_map/psum | solution.py:34
  74.4 0.9 %broadcast_multiply_fusion = f32[256,512]{1,0:T(8,128)} fusion(f32[256,512]{1,0:T(8,128)S(1)} %get-tuple-element.6, f32[512]{0:T(512)S(1)} %broadcast_divide_fusion), kind=kLoop, calls=%fused_computation.4 | loop fusion | flops 131072 | bytes 1050624 | tf_op jit(solution)/shard_map/mul | solution.py:36
  (16 shorter events, 0.1 us)
Async XLA Ops:
  6.5 47.5 %copy-start = (bf16[256,512]{1,0:T(8,128)(2,1)S(1)}, bf16[256,512]{1,0:T(8,128)(2,1)}, u32[]{:S(2)}) copy-start(bf16[256,512]{1,0:T(8,128)(2,1)} %param.3) | copy-start | bytes 786436
  6.5 50.3 %all-gather.2.cloned.1.call-start = ((), (), s32[]{:S(2)}) async-start(), calls=%async_computation | async-start | bytes 1310720 | tf_op jit(solution)/shard_map/all_gather | solution.py:27
  8.3 18.3 %copy-start.1 = (bf16[256,512]{1,0:T(8,128)(2,1)}, bf16[256,512]{1,0:T(8,128)(2,1)S(1)}, u32[]{:S(2)}) copy-start(bf16[256,512]{1,0:T(8,128)(2,1)S(1)} %broadcast_multiply_fusion.1) | copy-start | bytes 786436
  8.3 8.6 %collective-permute-start = (bf16[256,512]{1,0:T(8,128)(2,1)S(1)}, bf16[256,512]{1,0:T(8,128)(2,1)S(1)}, u32[]{:S(2)}, u32[]{:S(2)}) collective-permute-start(bf16[256,512]{1,0:T(8,128)(2,1)S(1)} %broadcast_multiply_fusion.1), channel_id=1, source_target_pairs={{0,4},{4,8},{8,12},{12,16},{16,20},{20,24},{24,28},{28,0},{1,5},{5... | collective-permute-start | bytes 786440 | tf_op jit(solution)/shard_map/ppermute | solution.py:15
  16.9 9.6 %collective-permute-start.1 = (bf16[256,512]{1,0:T(8,128)(2,1)S(1)}, bf16[256,512]{1,0:T(8,128)(2,1)S(1)}, u32[]{:S(2)}, u32[]{:S(2)}) collective-permute-start(bf16[256,512]{1,0:T(8,128)(2,1)S(1)} %collective-permute-done), channel_id=1, source_target_pairs={{0,4},{4,8},{8,12},{12,16},{16,20},{20,24},{24,28},{28,0},{1,5},{5... | collective-permute-start | bytes 786440 | tf_op jit(solution)/shard_map/ppermute | solution.py:15
  16.9 9.7 %collective-permute-start.4 = (bf16[256,512]{1,0:T(8,128)(2,1)S(1)}, bf16[256,512]{1,0:T(8,128)(2,1)S(1)}, u32[]{:S(2)}, u32[]{:S(2)}) collective-permute-start(bf16[256,512]{1,0:T(8,128)(2,1)S(1)} %broadcast_multiply_fusion.1), channel_id=1, source_target_pairs={{0,28},{4,0},{8,4},{12,8},{16,12},{20,16},{24,20},{28,24},{1,29},{... | collective-permute-start | bytes 786440 | tf_op jit(solution)/shard_map/ppermute | solution.py:17
  26.5 9.7 %collective-permute-start.2 = (bf16[256,512]{1,0:T(8,128)(2,1)S(1)}, bf16[256,512]{1,0:T(8,128)(2,1)S(1)}, u32[]{:S(2)}, u32[]{:S(2)}) collective-permute-start(bf16[256,512]{1,0:T(8,128)(2,1)S(1)} %collective-permute-done.1), channel_id=1, source_target_pairs={{0,4},{4,8},{8,12},{12,16},{16,20},{20,24},{24,28},{28,0},{1,5},{5... | collective-permute-start | bytes 786440 | tf_op jit(solution)/shard_map/ppermute | solution.py:15
  26.6 10.4 %collective-permute-start.5 = (bf16[256,512]{1,0:T(8,128)(2,1)S(1)}, bf16[256,512]{1,0:T(8,128)(2,1)S(1)}, u32[]{:S(2)}, u32[]{:S(2)}) collective-permute-start(bf16[256,512]{1,0:T(8,128)(2,1)S(1)} %collective-permute-done.4), channel_id=1, source_target_pairs={{0,28},{4,0},{8,4},{12,8},{16,12},{20,16},{24,20},{28,24},{1,29},{... | collective-permute-start | bytes 786440 | tf_op jit(solution)/shard_map/ppermute | solution.py:17
  36.3 8.1 %collective-permute-start.3 = (bf16[256,512]{1,0:T(8,128)(2,1)S(1)}, bf16[256,512]{1,0:T(8,128)(2,1)S(1)}, u32[]{:S(2)}, u32[]{:S(2)}) collective-permute-start(bf16[256,512]{1,0:T(8,128)(2,1)S(1)} %collective-permute-done.2), channel_id=1, source_target_pairs={{0,4},{4,8},{8,12},{12,16},{16,20},{20,24},{24,28},{28,0},{1,5},{5... | collective-permute-start | bytes 786440 | tf_op jit(solution)/shard_map/ppermute | solution.py:15
  37.0 13.4 %collective-permute-start.6 = (bf16[256,512]{1,0:T(8,128)(2,1)S(1)}, bf16[256,512]{1,0:T(8,128)(2,1)S(1)}, u32[]{:S(2)}, u32[]{:S(2)}) collective-permute-start(bf16[256,512]{1,0:T(8,128)(2,1)S(1)} %collective-permute-done.5), channel_id=1, source_target_pairs={{0,28},{4,0},{8,4},{12,8},{16,12},{20,16},{24,20},{28,24},{1,29},{... | collective-permute-start | bytes 786440 | tf_op jit(solution)/shard_map/ppermute | solution.py:17
Sparse Core Ops, SparseCore 0:
  26.7 28.6 all-gather.1
